TPU v7x, 32 devices: a whole 2x2x4 slice. The times are simulated.
32 devices in a mesh: ctx: 4 (over z), head: 8 (over y, x, core).
Axes of the slice: x: 2, y: 2, z: 4, core: 2. Of those that a mesh axis runs over, the one named last changes fastest.
Arguments:
- query_rows: bfloat16 [8192, 4096], P('ctx', 'head'), may hold values from -6 to 6
- key_rows: bfloat16 [8192, 4096], P('ctx', 'head'), may hold values from -6 to 6
- value_rows: bfloat16 [8192, 4096], P('ctx', 'head'), may hold values from -6 to 6
- out_grad: bfloat16 [8192, 4096], P('ctx', 'head'), may hold values from -6 to 6
- hub_blocks: int32 [2], replicated, may hold values from 0 to 63, as said below
- local_lists: int32 [64, 6], replicated, may hold values from -3 to 3
Outputs:
- attended: bfloat16 [8192, 4096], P('ctx', 'head')
- query_gradient: bfloat16 [8192, 4096], P('ctx', 'head')
- key_grad: bfloat16 [8192, 4096], P('ctx', 'head')
- value_grad: bfloat16 [8192, 4096], P('ctx', 'head')
Inputs may be any that keep to these rules, and one draw needn't show every extreme that they name: `hub_blocks`: 2 distinct block numbers.
All inputs are finite; a program needn't handle non-finite values.
Results may differ from a plain program's by a relative error of at most 0.012.
The roundings to bfloat16 on the way count: a program that leaves them out, or rounds other values in their place, can miss the bound.
Values may be sent and summed in bfloat16 or wider, within the bound.
A program may use at most 192 MiB of HBM per device.

v0:
```python
import math
import jax
import jax.numpy as jnp
from jax import lax
from jax.sharding import PartitionSpec as P

DH = 128
BLK = 128
HB = 3
G = 2


def padded_2(cells, sides, width):
    for axis, dim in sides:
        count = lax.axis_size(axis)
        ends = count - 1
        head = lax.slice_in_dim(cells, 0, width, axis=dim)
        tail = lax.slice_in_dim(cells, cells.shape[dim] - width, cells.shape[dim], axis=dim)
        cells = jnp.concatenate(
            [
                lax.ppermute(tail, axis, [(i, (i + 1) % count) for i in range(ends)]),
                cells,
                lax.ppermute(head, axis, [((i + 1) % count, i) for i in range(ends)]),
            ],
            axis=dim,
        )
    return cells


def entry_table(block_lists, positions, first_block, total_blocks, extended):
    global_block = first_block - HB + positions
    query_inside = (global_block >= 0) & (global_block < total_blocks)
    key_spot = positions[:, None] + block_lists
    key_global = global_block[:, None] + block_lists
    living = query_inside[:, None] & (key_global >= 0) & (key_global < total_blocks)
    living = living & (key_spot >= 0) & (key_spot < extended)
    set_count = positions.shape[0]
    hub_spots = jnp.broadcast_to(extended + jnp.arange(G, dtype=jnp.int32)[None, :], (set_count, G))
    entries = jnp.concatenate([jnp.clip(key_spot, 0, extended - 1), hub_spots], axis=1)
    all_living = jnp.concatenate(
        [living, jnp.broadcast_to(query_inside[:, None], (set_count, G))], axis=1
    )
    return (entries, all_living)


def grouped(source):
    return source.reshape((source.shape[0] // 4, 4) + source.shape[1:])


def block_scores(query_group, entries, living, key_store, score_scale):
    gathered = key_store[entries]
    logit_scores = (
        jnp.einsum("bqhd,bekhd->bhqek", query_group, gathered, preferred_element_type=jnp.float32)
        * score_scale
    )
    logit_scores = jnp.where(living[:, None, None, :, None], logit_scores, -1e30)
    return (logit_scores, gathered)


def local(query_rows, key_rows, value_rows, out_grad, hub_blocks, local_lists):
    score_scale = 1.0 / math.sqrt(DH)
    ctx_count = lax.axis_size("ctx")
    position = lax.axis_index("ctx")
    tok_rows, columns = query_rows.shape
    head_count = columns // DH
    blocks_here = tok_rows // BLK
    total_blocks = blocks_here * ctx_count
    extended = blocks_here + 2 * HB
    first_block = position * blocks_here
    padded_lists = jnp.pad(local_lists, ((HB, HB), (0, 0)))
    ext_lists = lax.dynamic_slice_in_dim(padded_lists, first_block, extended, 0)
    positions = jnp.arange(extended, dtype=jnp.int32)
    joined = jnp.concatenate([key_rows, value_rows], axis=1)
    widened = padded_2(joined, (("ctx", 0),), HB * BLK)
    far_keys = widened[:, :columns]
    far_values = widened[:, columns : 2 * columns]
    hub_spot = hub_blocks - first_block
    hub_picks = hub_spot[:, None] == jnp.arange(blocks_here, dtype=jnp.int32)[None, :]
    hub_term = jnp.dot(
        hub_picks.astype(jnp.bfloat16),
        joined.reshape(blocks_here, BLK * 2 * columns),
        preferred_element_type=jnp.float32,
    )
    hub_store = lax.psum(hub_term.astype(jnp.bfloat16), "ctx").reshape(G * BLK, 2 * columns)
    key_store = jnp.concatenate([far_keys, hub_store[:, :columns]], axis=0).reshape(
        extended + G, BLK, head_count, DH
    )
    value_store = jnp.concatenate([far_values, hub_store[:, columns:]], axis=0).reshape(
        extended + G, BLK, head_count, DH
    )
    local_entries, local_living = entry_table(
        ext_lists[HB : HB + blocks_here],
        positions[HB : HB + blocks_here],
        first_block,
        total_blocks,
        extended,
    )
    query_blocks = query_rows.reshape(blocks_here, BLK, head_count, DH)
    grad_blocks = out_grad.reshape(blocks_here, BLK, head_count, DH)

    def forward_group(members):
        query_group, entries, living = members
        logit_scores, gathered = block_scores(query_group, entries, living, key_store, score_scale)
        highest = jnp.max(logit_scores, axis=(3, 4), keepdims=True)
        log_norm = highest + jnp.log(
            jnp.sum(jnp.exp(logit_scores - highest), axis=(3, 4), keepdims=True)
        )
        weights = jnp.exp(logit_scores - log_norm).astype(jnp.bfloat16)
        mixed = jnp.einsum(
            "bhqek,bekhd->bqhd", weights, value_store[entries], preferred_element_type=jnp.float32
        )
        return (mixed.astype(jnp.bfloat16), log_norm[:, :, :, 0, 0])

    mixed, norms = lax.map(
        forward_group, (grouped(query_blocks), grouped(local_entries), grouped(local_living))
    )
    attended = mixed.reshape(tok_rows, columns)
    log_norms = norms.reshape(blocks_here, head_count, BLK)
    offsets = jnp.sum(
        grad_blocks.astype(jnp.float32)
        * attended.reshape(blocks_here, BLK, head_count, DH).astype(jnp.float32),
        axis=3,
    )
    offsets = jnp.transpose(offsets, (0, 2, 1))
    set_norms, set_offsets = (log_norms, offsets)
    set_queries, set_grads = (query_blocks, grad_blocks)
    set_entries, set_living = (local_entries, local_living)
    store_rows = extended + G
    store_ids = jnp.arange(store_rows, dtype=jnp.int32)

    def grad_group(carry, members):
        key_acc, value_acc = carry
        query_group, pushed_rows, norm_group, offset_group, entries, living = members
        logit_scores, gathered = block_scores(query_group, entries, living, key_store, score_scale)
        chances = jnp.exp(logit_scores - norm_group[:, :, :, None, None])
        weights = chances.astype(jnp.bfloat16)
        shifted_entries = jnp.einsum(
            "bqhd,bekhd->bhqek",
            pushed_rows,
            value_store[entries],
            preferred_element_type=jnp.float32,
        )
        decay_slopes = (
            chances * (shifted_entries - offset_group[:, :, :, None, None]) * score_scale
        ).astype(jnp.bfloat16)
        query_part = jnp.einsum(
            "bhqek,bekhd->bqhd", decay_slopes, gathered, preferred_element_type=jnp.float32
        )
        key_part = jnp.einsum(
            "bhqek,bqhd->bekhd", decay_slopes, query_group, preferred_element_type=jnp.float32
        )
        value_part = jnp.einsum(
            "bhqek,bqhd->bekhd", weights, pushed_rows, preferred_element_type=jnp.float32
        )
        spots = (
            ((entries[:, :, None] == store_ids[None, None, :]) & living[:, :, None])
            .astype(jnp.float32)
            .reshape(-1, store_rows)
        )
        key_acc = key_acc + jnp.dot(
            spots.T, key_part.reshape(spots.shape[0], -1), precision=lax.Precision.HIGHEST
        )
        value_acc = value_acc + jnp.dot(
            spots.T, value_part.reshape(spots.shape[0], -1), precision=lax.Precision.HIGHEST
        )
        return ((key_acc, value_acc), query_part)

    empty_acc = jnp.zeros((store_rows, BLK * columns), jnp.float32)
    (key_acc, value_acc), query_parts = lax.scan(
        grad_group,
        (empty_acc, empty_acc),
        (
            grouped(set_queries),
            grouped(set_grads),
            grouped(set_norms),
            grouped(set_offsets),
            grouped(set_entries),
            grouped(set_living),
        ),
    )
    query_gradient = (
        query_parts.reshape(-1, BLK, head_count, DH).reshape(tok_rows, columns).astype(jnp.bfloat16)
    )
    gradients = jnp.concatenate([key_acc, value_acc], axis=1)
    owned_rows = gradients[HB : HB + blocks_here]
    rim_rows = jnp.concatenate([gradients[:HB], gradients[HB + blocks_here : extended]], axis=0)
    returned = padded_2(rim_rows.astype(jnp.bfloat16), (("ctx", 0),), HB).astype(rim_rows.dtype)
    owned_rows = owned_rows.at[:HB].add(returned[:HB])
    owned_rows = owned_rows.at[blocks_here - HB :].add(returned[3 * HB :])
    hub_total = lax.psum(gradients[extended : extended + G], "ctx")
    owned_rows = owned_rows + jnp.dot(
        hub_picks.T.astype(jnp.float32), hub_total, precision=lax.Precision.HIGHEST
    )
    key_grad = owned_rows[:, : BLK * columns].reshape(tok_rows, columns).astype(jnp.bfloat16)
    value_grad = owned_rows[:, BLK * columns :].reshape(tok_rows, columns).astype(jnp.bfloat16)
    return (attended, query_gradient, key_grad, value_grad)


def solution(mesh):
    return jax.shard_map(
        local,
        mesh=mesh,
        in_specs=(P("ctx", "head"), P("ctx", "head"), P("ctx", "head"), P("ctx", "head"), P(), P()),
        out_specs=(P("ctx", "head"), P("ctx", "head"), P("ctx", "head"), P("ctx", "head")),
        check_vma=False,
    )
```

profile of v0, /device:TPU:0, one launch (start us, length us, event | category | flops | bytes accessed | tf_op | source)
XLA Modules:
  0.0 707.2 jit_solution(10489579091226312188)
XLA Ops:
  44.7 26.4 %all-reduce.4.cloned.1.call-done = bf16[256,1024]{1,0:T(8,128)(2,1)} async-done(((bf16[256,1024]{1,0:T(8,128)(2,1)}), bf16[256,1024]{1,0:T(8,128)(2,1)}) %all-reduce.4.cloned.1.call-update) | async-done | bytes 524304 | tf_op jit(solution)/shard_map/psum | solution.py:84
  92.2 99.9 %while.29 = (s32[]{:T(128)}, bf16[4,4,128,4,128]{2,4,3,1,0:T(8,128)(2,1)}, f32[4,4,4,128]{3,2,1,0:T(4,128)S(1)}, s32[4,4,8]{2,1,0:T(4,128)S(1)}, bf16[24,128,4,1...) while((s32[]{:T(128)}, ...), condition=%wide.region_4.5_spmd, body=%wide.region_1.4_spmd.sunk | while | flops 1097071744 | bytes 76616880 | solution.py:114
  123.4 7.6 %gather_fusion = bf16[32,128,4,128]{3,2,1,0:T(4,128)(2,1)} fusion(bf16[24,128,4,128]{3,2,1,0:T(4,128)(2,1)} %get-tuple-element.451, s32[1024]{0:T(1024)S(1)} %pad_clamp_fusion.4), kind=kCustom, calls=%fused_computation.1.clone.1 | custom fusion | bytes 8388736 | tf_op jit(solution)/shard_map/while/body/eval_jaxpr/gather | solution.py:51
  195.7 394.1 %while.30 = (s32[]{:T(128)}, f32[24,65536]{1,0:T(8,128)}, f32[24,65536]{1,0:T(8,128)}, bf16[4,4,128,4,128]{2,4,3,1,0:T(8,128)(2,1)}, s32[4,4,8]{2,1,0:T(4,128)S(...) while((s32[]{:T(128)}, f32[24,65536]{1,0:T(8,128)}, ...), condition=%wide.region_7.8_spmd.clone, body=%wide.region_6.7_spmd.clone.sunk | while | flops 3921678336 | bytes 274790528 | solution.py:169
  233.1 9.9 %copy.107 = f32[4,8,128,4,128]{4,3,2,1,0:T(4,128)} copy(f32[4,8,128,4,128]{2,4,1,3,0:T(8,128)} %fusion.115) | data formatting | bytes 16777216 | tf_op jit(solution)/shard_map/while/body/eval_jaxpr/bhqek,bqhd->bekhd/transpose | solution.py:152
  243.0 9.0 %reshape.295 = f32[32,65536]{1,0:T(8,128)} reshape(f32[4,8,128,4,128]{4,3,2,1,0:T(4,128)} %copy.107) | data formatting | bytes 16777216 | tf_op jit(solution)/shard_map/while/body/eval_jaxpr/reshape | solution.py:164
  252.1 8.3 %convolution_add_fusion.6 = f32[24,65536]{1,0:T(8,128)} fusion(f32[32,65536]{1,0:T(8,128)} %reshape.295, f32[24,65536]{1,0:T(8,128)} %get-tuple-element.469, pred[]{:T(512)S(6)} %compare.14, s32[32]{0:T(128)S(1)} %eq.72, pred[32]{0:T(512)(128)(4,1)S(1)} %and.73), kind=kOutput, calls=%fused_computation.30.clone.1 | convolution fusion | flops 607127040 | bytes 20971680 | tf_op jit(solution)/shard_map/while/body/eval_jaxpr/dot_general | solution.py:163
  265.9 9.9 %copy.106 = f32[4,8,128,4,128]{4,3,2,1,0:T(4,128)} copy(f32[4,8,128,4,128]{2,4,1,3,0:T(8,128)} %convolution_bitcast_fusion.3) | data formatting | bytes 16777216 | tf_op jit(solution)/shard_map/while/body/eval_jaxpr/bhqek,bqhd->bekhd/transpose | solution.py:149
  275.8 9.0 %reshape.294 = f32[32,65536]{1,0:T(8,128)} reshape(f32[4,8,128,4,128]{4,3,2,1,0:T(4,128)} %copy.106) | data formatting | bytes 16777216 | tf_op jit(solution)/shard_map/while/body/eval_jaxpr/reshape | solution.py:161
  284.9 8.0 %convolution_add_fusion.5 = f32[24,65536]{1,0:T(8,128)} fusion(f32[32,65536]{1,0:T(8,128)} %reshape.294, f32[24,65536]{1,0:T(8,128)} %get-tuple-element.468, pred[]{:T(512)S(6)} %compare.14, s32[32]{0:T(128)S(1)} %eq.72, pred[32]{0:T(512)(128)(4,1)S(1)} %and.73), kind=kOutput, calls=%fused_computation.31.clone.1 | convolution fusion | flops 607127040 | bytes 20971680 | tf_op jit(solution)/shard_map/while/body/eval_jaxpr/dot_general | solution.py:160
  330.1 9.9 %copy.107 = f32[4,8,128,4,128]{4,3,2,1,0:T(4,128)} copy(f32[4,8,128,4,128]{2,4,1,3,0:T(8,128)} %fusion.115) | data formatting | bytes 16777216 | tf_op jit(solution)/shard_map/while/body/eval_jaxpr/bhqek,bqhd->bekhd/transpose | solution.py:152
  340.0 9.0 %reshape.295 = f32[32,65536]{1,0:T(8,128)} reshape(f32[4,8,128,4,128]{4,3,2,1,0:T(4,128)} %copy.107) | data formatting | bytes 16777216 | tf_op jit(solution)/shard_map/while/body/eval_jaxpr/reshape | solution.py:164
  349.0 9.2 %convolution_add_fusion.6 = f32[24,65536]{1,0:T(8,128)} fusion(f32[32,65536]{1,0:T(8,128)} %reshape.295, f32[24,65536]{1,0:T(8,128)} %get-tuple-element.469, pred[]{:T(512)S(6)} %compare.14, s32[32]{0:T(128)S(1)} %eq.72, pred[32]{0:T(512)(128)(4,1)S(1)} %and.73), kind=kOutput, calls=%fused_computation.30.clone.1 | convolution fusion | flops 607127040 | bytes 20971680 | tf_op jit(solution)/shard_map/while/body/eval_jaxpr/dot_general | solution.py:163
  363.8 9.9 %copy.106 = f32[4,8,128,4,128]{4,3,2,1,0:T(4,128)} copy(f32[4,8,128,4,128]{2,4,1,3,0:T(8,128)} %convolution_bitcast_fusion.3) | data formatting | bytes 16777216 | tf_op jit(solution)/shard_map/while/body/eval_jaxpr/bhqek,bqhd->bekhd/transpose | solution.py:149
  373.8 9.0 %reshape.294 = f32[32,65536]{1,0:T(8,128)} reshape(f32[4,8,128,4,128]{4,3,2,1,0:T(4,128)} %copy.106) | data formatting | bytes 16777216 | tf_op jit(solution)/shard_map/while/body/eval_jaxpr/reshape | solution.py:161
  382.8 9.0 %convolution_add_fusion.5 = f32[24,65536]{1,0:T(8,128)} fusion(f32[32,65536]{1,0:T(8,128)} %reshape.294, f32[24,65536]{1,0:T(8,128)} %get-tuple-element.468, pred[]{:T(512)S(6)} %compare.14, s32[32]{0:T(128)S(1)} %eq.72, pred[32]{0:T(512)(128)(4,1)S(1)} %and.73), kind=kOutput, calls=%fused_computation.31.clone.1 | convolution fusion | flops 607127040 | bytes 20971680 | tf_op jit(solution)/shard_map/while/body/eval_jaxpr/dot_general | solution.py:160
  429.0 9.9 %copy.107 = f32[4,8,128,4,128]{4,3,2,1,0:T(4,128)} copy(f32[4,8,128,4,128]{2,4,1,3,0:T(8,128)} %fusion.115) | data formatting | bytes 16777216 | tf_op jit(solution)/shard_map/while/body/eval_jaxpr/bhqek,bqhd->bekhd/transpose | solution.py:152
  438.9 9.0 %reshape.295 = f32[32,65536]{1,0:T(8,128)} reshape(f32[4,8,128,4,128]{4,3,2,1,0:T(4,128)} %copy.107) | data formatting | bytes 16777216 | tf_op jit(solution)/shard_map/while/body/eval_jaxpr/reshape | solution.py:164
  447.9 9.2 %convolution_add_fusion.6 = f32[24,65536]{1,0:T(8,128)} fusion(f32[32,65536]{1,0:T(8,128)} %reshape.295, f32[24,65536]{1,0:T(8,128)} %get-tuple-element.469, pred[]{:T(512)S(6)} %compare.14, s32[32]{0:T(128)S(1)} %eq.72, pred[32]{0:T(512)(128)(4,1)S(1)} %and.73), kind=kOutput, calls=%fused_computation.30.clone.1 | convolution fusion | flops 607127040 | bytes 20971680 | tf_op jit(solution)/shard_map/while/body/eval_jaxpr/dot_general | solution.py:163
  462.8 9.9 %copy.106 = f32[4,8,128,4,128]{4,3,2,1,0:T(4,128)} copy(f32[4,8,128,4,128]{2,4,1,3,0:T(8,128)} %convolution_bitcast_fusion.3) | data formatting | bytes 16777216 | tf_op jit(solution)/shard_map/while/body/eval_jaxpr/bhqek,bqhd->bekhd/transpose | solution.py:149
  472.7 9.0 %reshape.294 = f32[32,65536]{1,0:T(8,128)} reshape(f32[4,8,128,4,128]{4,3,2,1,0:T(4,128)} %copy.106) | data formatting | bytes 16777216 | tf_op jit(solution)/shard_map/while/body/eval_jaxpr/reshape | solution.py:161
  481.7 9.0 %convolution_add_fusion.5 = f32[24,65536]{1,0:T(8,128)} fusion(f32[32,65536]{1,0:T(8,128)} %reshape.294, f32[24,65536]{1,0:T(8,128)} %get-tuple-element.468, pred[]{:T(512)S(6)} %compare.14, s32[32]{0:T(128)S(1)} %eq.72, pred[32]{0:T(512)(128)(4,1)S(1)} %and.73), kind=kOutput, calls=%fused_computation.31.clone.1 | convolution fusion | flops 607127040 | bytes 20971680 | tf_op jit(solution)/shard_map/while/body/eval_jaxpr/dot_general | solution.py:160
  527.9 9.9 %copy.107 = f32[4,8,128,4,128]{4,3,2,1,0:T(4,128)} copy(f32[4,8,128,4,128]{2,4,1,3,0:T(8,128)} %fusion.115) | data formatting | bytes 16777216 | tf_op jit(solution)/shard_map/while/body/eval_jaxpr/bhqek,bqhd->bekhd/transpose | solution.py:152
  537.8 9.0 %reshape.295 = f32[32,65536]{1,0:T(8,128)} reshape(f32[4,8,128,4,128]{4,3,2,1,0:T(4,128)} %copy.107) | data formatting | bytes 16777216 | tf_op jit(solution)/shard_map/while/body/eval_jaxpr/reshape | solution.py:164
  546.8 9.2 %convolution_add_fusion.6 = f32[24,65536]{1,0:T(8,128)} fusion(f32[32,65536]{1,0:T(8,128)} %reshape.295, f32[24,65536]{1,0:T(8,128)} %get-tuple-element.469, pred[]{:T(512)S(6)} %compare.14, s32[32]{0:T(128)S(1)} %eq.72, pred[32]{0:T(512)(128)(4,1)S(1)} %and.73), kind=kOutput, calls=%fused_computation.30.clone.1 | convolution fusion | flops 607127040 | bytes 20971680 | tf_op jit(solution)/shard_map/while/body/eval_jaxpr/dot_general | solution.py:163
  561.6 9.9 %copy.106 = f32[4,8,128,4,128]{4,3,2,1,0:T(4,128)} copy(f32[4,8,128,4,128]{2,4,1,3,0:T(8,128)} %convolution_bitcast_fusion.3) | data formatting | bytes 16777216 | tf_op jit(solution)/shard_map/while/body/eval_jaxpr/bhqek,bqhd->bekhd/transpose | solution.py:149
  571.6 9.0 %reshape.294 = f32[32,65536]{1,0:T(8,128)} reshape(f32[4,8,128,4,128]{4,3,2,1,0:T(4,128)} %copy.106) | data formatting | bytes 16777216 | tf_op jit(solution)/shard_map/while/body/eval_jaxpr/reshape | solution.py:161
  580.6 9.0 %convolution_add_fusion.5 = f32[24,65536]{1,0:T(8,128)} fusion(f32[32,65536]{1,0:T(8,128)} %reshape.294, f32[24,65536]{1,0:T(8,128)} %get-tuple-element.468, pred[]{:T(512)S(6)} %compare.14, s32[32]{0:T(128)S(1)} %eq.72, pred[32]{0:T(512)(128)(4,1)S(1)} %and.73), kind=kOutput, calls=%fused_computation.31.clone.1 | convolution fusion | flops 607127040 | bytes 20971680 | tf_op jit(solution)/shard_map/while/body/eval_jaxpr/dot_general | solution.py:160
  617.9 8.4 %slice.127 = f32[16,131072]{1,0:T(8,128)} slice(f32[24,131072]{1,0:T(8,128)} %constant_dynamic-update-slice_fusion.2), slice={[3:19], [0:131072]} | slice | bytes 16777216 | tf_op jit(solution)/shard_map/slice | solution.py:185
  638.9 20.5 %scatter-add.6 = f32[16,131072]{1,0:T(8,128)} dynamic-update-slice(f32[16,131072]{1,0:T(8,128)} %slice.127, f32[3,131072]{1,0:T(4,128)S(1)} %convert_add_fusion, s32[]{:T(128)} %constant.122.clone.1, s32[]{:T(128)} %constant.122.clone.1) | dynamic-update-slice | bytes 3145732 | tf_op jit(solution)/shard_map/scatter-add | solution.py:188
  663.6 13.4 %scatter-add.9 = f32[16,131072]{1,0:T(8,128)} dynamic-update-slice(f32[16,131072]{1,0:T(8,128)} %scatter-add.6, f32[3,131072]{1,0:T(4,128)S(1)} %slice_add_fusion, s32[]{:T(128)} %constant.132.clone.1, s32[]{:T(128)} %constant.122.clone.1) | dynamic-update-slice | bytes 3145732 | tf_op jit(solution)/shard_map/scatter-add | solution.py:189
  677.1 9.4 %all-reduce.6.cloned.1.call-done = f32[2,131072]{1,0:T(2,128)} async-done(((f32[2,131072]{1,0:T(2,128)}), f32[2,131072]{1,0:T(2,128)}) %all-reduce.6.cloned.1.call-update) | async-done | bytes 1048592 | tf_op jit(solution)/shard_map/psum | solution.py:190
  (242 shorter events, 382.9 us)
Async XLA Ops:
  7.2 2.2 copy-start.8
  7.2 63.9 %all-reduce.4.cloned.1.call-start = ((), (), s32[]{:S(2)}) async-start(), calls=%async_computation | async-start | bytes 1048576 | tf_op jit(solution)/shard_map/psum | solution.py:84
  13.0 59.1 %collective-permute-start = (bf16[384,1024]{1,0:T(8,128)(2,1)}, bf16[384,1024]{1,0:T(8,128)(2,1)S(1)}, u32[]{:S(2)}, u32[]{:S(2)}) collective-permute-start(bf16[384,1024]{1,0:T(8,128)(2,1)} %get-tuple-element.282), channel_id=1, source_target_pairs={{0,8},{8,16},{16,24},{1,9},{9,17},{17,25},{2,10},{10,18},{18,26},{... | collective-permute-start | bytes 2359304 | tf_op jit(solution)/shard_map/ppermute | solution.py:21
  18.0 54.1 %collective-permute-start.1 = (bf16[384,1024]{1,0:T(8,128)(2,1)}, bf16[384,1024]{1,0:T(8,128)(2,1)}, u32[]{:S(2)}, u32[]{:S(2)}) collective-permute-start(bf16[384,1024]{1,0:T(8,128)(2,1)} %get-tuple-element.283), channel_id=1, source_target_pairs={{8,0},{16,8},{24,16},{9,1},{17,9},{25,17},{10,2},{18,10},{26,18},{... | collective-permute-start | bytes 2359304 | tf_op jit(solution)/shard_map/ppermute | solution.py:23
  19.3 4.8 copy-start.12
  24.1 5.0 copy-start.7
  29.1 657.4 %all-reduce.6.cloned.1.call-start = ((), (), s32[]{:S(2)}) async-start(), calls=%async_computation.1 | async-start | bytes 2097152 | tf_op jit(solution)/shard_map/psum | solution.py:190
  31.2 3.3 copy-start.9
  111.8 2.2 copy-start.3
  136.6 2.2 copy-start.3
  186.3 2.2 copy-start.3
  219.1 3.7 copy-start.4
  219.1 3.8 copy-start.5
  222.9 3.5 copy-start
  252.0 8.3 %copy-start.2 = (bf16[4,4,128,8,128]{4,2,3,1,0:T(8,128)(2,1)S(1)}, bf16[4,4,128,8,128]{4,2,3,1,0:T(8,128)(2,1)}, u32[]{:S(2)}) copy-start(bf16[4,4,128,8,128]{4,2,3,1,0:T(8,128)(2,1)} %copy-done.1) | copy-start | bytes 12582916 | tf_op jit(solution)/shard_map/while
  316.1 3.7 copy-start.4
  316.1 3.8 copy-start.5
  319.9 3.5 copy-start
  349.0 9.2 %copy-start.2 = (bf16[4,4,128,8,128]{4,2,3,1,0:T(8,128)(2,1)S(1)}, bf16[4,4,128,8,128]{4,2,3,1,0:T(8,128)(2,1)}, u32[]{:S(2)}) copy-start(bf16[4,4,128,8,128]{4,2,3,1,0:T(8,128)(2,1)} %copy-done.1) | copy-start | bytes 12582916 | tf_op jit(solution)/shard_map/while
  415.0 3.7 copy-start.4
  415.0 3.8 copy-start.5
  418.8 3.5 copy-start
  447.9 9.2 %copy-start.2 = (bf16[4,4,128,8,128]{4,2,3,1,0:T(8,128)(2,1)S(1)}, bf16[4,4,128,8,128]{4,2,3,1,0:T(8,128)(2,1)}, u32[]{:S(2)}) copy-start(bf16[4,4,128,8,128]{4,2,3,1,0:T(8,128)(2,1)} %copy-done.1) | copy-start | bytes 12582916 | tf_op jit(solution)/shard_map/while
  513.9 3.7 copy-start.4
  513.9 3.8 copy-start.5
  517.7 3.5 copy-start
  546.8 9.2 %copy-start.2 = (bf16[4,4,128,8,128]{4,2,3,1,0:T(8,128)(2,1)S(1)}, bf16[4,4,128,8,128]{4,2,3,1,0:T(8,128)(2,1)}, u32[]{:S(2)}) copy-start(bf16[4,4,128,8,128]{4,2,3,1,0:T(8,128)(2,1)} %copy-done.1) | copy-start | bytes 12582916 | tf_op jit(solution)/shard_map/while
  589.8 6.1 slice-start
  589.8 6.1 slice-start.1
  606.3 26.6 %collective-permute-start.2 = (bf16[3,131072]{1,0:T(4,128)(2,1)}, bf16[3,131072]{1,0:T(4,128)(2,1)S(1)}, u32[]{:S(2)}, u32[]{:S(2)}) collective-permute-start(bf16[3,131072]{1,0:T(4,128)(2,1)} %get-tuple-element.276), channel_id=1, source_target_pairs={{0,8},{8,16},{16,24},{1,9},{9,17},{17,25},{2,10},{10,18},{18,26},{... | collective-permute-start | bytes 2359304 | tf_op jit(solution)/shard_map/ppermute | solution.py:21
  610.0 24.7 %collective-permute-start.3 = (bf16[3,131072]{1,0:T(4,128)(2,1)}, bf16[3,131072]{1,0:T(4,128)(2,1)}, u32[]{:S(2)}, u32[]{:S(2)}) collective-permute-start(bf16[3,131072]{1,0:T(4,128)(2,1)} %get-tuple-element.277), channel_id=1, source_target_pairs={{8,0},{16,8},{24,16},{9,1},{17,9},{25,17},{10,2},{18,10},{26,18},{... | collective-permute-start | bytes 2359304 | tf_op jit(solution)/shard_map/ppermute | solution.py:23
  663.6 22.9 %copy-start.11 = (s32[2]{0:T(128)S(1)}, s32[2]{0:T(128)}, u32[]{:S(2)}) copy-start(s32[2]{0:T(128)} %copy-done.10) | copy-start | bytes 28
  (7 other events, 13.5 us)
Sparse Core Ops, SparseCore 0:
  29.2 41.8 all-reduce.3
  633.0 53.5 all-reduce.5
where the time goes:
time: 718 us; the launch traced here: 707 us
  local copies, waits for them, and re-layouts  424 us (59%)
  matrix products  183 us (25%)
  waiting for transfers between devices  37.7 us (5%)
  other arithmetic  35.4 us (5%)
  between operations  14.6 us (2%)
  starting transfers between devices  11.3 us (2%)
    gather x16, local copies, waits for them, and re-layouts, block_scores(): gathered = key_store[entries]  104 us
    transpose x4, local copies, waits for them, and re-layouts, grad_group(): jnp.einsum('bhqek,bqhd->bekhd', weights, pushed_rows, preferred_element_t...  39.6 us
    transpose x4, local copies, waits for them, and re-layouts, grad_group(): jnp.einsum('bhqek,bqhd->bekhd', decay_slopes, query_group, preferred_elem...  39.6 us
    reshape x4, local copies, waits for them, and re-layouts, grad_group(): value_part.reshape(spots.shape[0], -1)  36.2 us
    reshape x4, local copies, waits for them, and re-layouts, grad_group(): key_part.reshape(spots.shape[0], -1)  36.2 us
    dot_general x4, matrix products, grad_group(): jnp.dot(spots.T, value_part.reshape(spots.shape[0], -1), precision=lax.Pr...  35.9 us
    dot_general x4, matrix products, grad_group(): jnp.dot(spots.T, key_part.reshape(spots.shape[0], -1), precision=lax.Prec...  35.1 us
    psum x1, waiting for transfers between devices, local(): lax.psum(hub_term.astype(jnp.bfloat16), 'ctx').reshape(G * BLK, 2 * columns)  26.4 us
  transfers between devices with their start and end apart: 6, of which 3 were waited for; matrix products, arithmetic and copies ran while one was open for 13% of the time, Pallas kernels for 0%

commit v1 on v0

--- a/solution.py
+++ b/solution.py
@@ -81,7 +81,9 @@
         joined.reshape(blocks_here, BLK * 2 * columns),
         preferred_element_type=jnp.float32,
     )
-    hub_store = lax.psum(hub_term.astype(jnp.bfloat16), "ctx").reshape(G * BLK, 2 * columns)
+    hub_store = jnp.sum(lax.all_gather(hub_term.astype(jnp.bfloat16), "ctx"), axis=0).reshape(
+        G * BLK, 2 * columns
+    )
     key_store = jnp.concatenate([far_keys, hub_store[:, :columns]], axis=0).reshape(
         extended + G, BLK, head_count, DH
     )

time: 718 us -> 749 us (1.043)
  loops' own time: 1.26 us -> 12.5 us
  waiting for transfers between devices: 37.7 us -> 48 us
    psum x1 -> x0, waiting for transfers between devices: 26.4 us -> none  [local(): lax.psum(hub_term.astype(jnp.bfloat16), 'ctx').reshape(G * BLK, 2 * columns)]
    ppermute x2, waiting for transfers between devices: 1.85 us -> 23.1 us  [padded_2(): lax.ppermute(head, axis, [((i + 1) % count, i) for i in range(ends)])]
    ppermute x2, waiting for transfers between devices: 0.01 us -> 14.9 us  [padded_2(): lax.ppermute(tail, axis, [(i, (i + 1) % count) for i in range(ends)])]
    another operation x1, loops' own time: 0.68 us -> 12.2 us  [local(): lax.scan(grad_group, (empty_acc, empty_acc), (grouped(set_queries), group...]
  transfers between devices with their start and end apart: 6 -> 6, of which waited for: 3 -> 3; matrix products, arithmetic and copies ran while one was open for 13% -> 12% of each run, Pallas kernels for 0% -> 0%
where the time goes in v1:
time: 749 us; the launch traced here: 736 us
  local copies, waits for them, and re-layouts  426 us (57%)
  matrix products  183 us (24%)
  waiting for transfers between devices  48 us (6%)
  other arithmetic  41.6 us (6%)
  between operations  14.7 us (2%)
  loops' own time  12.5 us (2%)
  starting transfers between devices  9.72 us (1%)
    gather x16, local copies, waits for them, and re-layouts, block_scores(): gathered = key_store[entries]  104 us
    transpose x4, local copies, waits for them, and re-layouts, grad_group(): jnp.einsum('bhqek,bqhd->bekhd', decay_slopes, query_group, preferred_elem...  39.7 us
    transpose x4, local copies, waits for them, and re-layouts, grad_group(): jnp.einsum('bhqek,bqhd->bekhd', weights, pushed_rows, preferred_element_t...  39.7 us
    reshape x4, local copies, waits for them, and re-layouts, grad_group(): key_part.reshape(spots.shape[0], -1)  36.1 us
    reshape x4, local copies, waits for them, and re-layouts, grad_group(): value_part.reshape(spots.shape[0], -1)  36.1 us
    dot_general x4, matrix products, grad_group(): jnp.dot(spots.T, value_part.reshape(spots.shape[0], -1), precision=lax.Pr...  35.9 us
    dot_general x4, matrix products, grad_group(): jnp.dot(spots.T, key_part.reshape(spots.shape[0], -1), precision=lax.Prec...  35.1 us
    ppermute x2, waiting for transfers between devices, padded_2(): lax.ppermute(head, axis, [((i + 1) % count, i) for i in range(ends)])  23.1 us
  transfers between devices with their start and end apart: 6, of which 3 were waited for; matrix products, arithmetic and copies ran while one was open for 12% of the time, Pallas kernels for 0%

profile of v1, /device:TPU:0, one launch (start us, length us, event | category | flops | bytes accessed | tf_op | source)
XLA Modules:
  0.0 736.0 jit_solution(16459749163349200230)
XLA Ops:
  45.3 14.9 %collective-permute-done = bf16[384,1024]{1,0:T(8,128)(2,1)S(1)} collective-permute-done((bf16[384,1024]{1,0:T(8,128)(2,1)}, bf16[384,1024]{1,0:T(8,128)(2,1)S(1)}, u32[]{:S(2)}, u32[]{:S(2)}) %collective-permute-start) | collective-permute-done | bytes 786464 | tf_op jit(solution)/shard_map/ppermute | solution.py:21
  60.2 23.1 %collective-permute-done.1 = bf16[384,1024]{1,0:T(8,128)(2,1)} collective-permute-done((bf16[384,1024]{1,0:T(8,128)(2,1)}, bf16[384,1024]{1,0:T(8,128)(2,1)}, u32[]{:S(2)}, u32[]{:S(2)}) %collective-permute-start.1) | collective-permute-done | bytes 786464 | tf_op jit(solution)/shard_map/ppermute | solution.py:23
  112.7 99.7 %while.29 = (s32[]{:T(128)}, bf16[4,4,128,4,128]{2,4,3,1,0:T(8,128)(2,1)}, f32[4,4,4,128]{3,2,1,0:T(4,128)S(1)}, s32[4,4,8]{2,1,0:T(4,128)S(1)}, bf16[24,128,4,1...) while((s32[]{:T(128)}, ...), condition=%wide.region_4.5_spmd, body=%wide.region_1.4_spmd.sunk | while | flops 1097071744 | bytes 76616880 | solution.py:116
  216.0 405.4 %while.30 = (s32[]{:T(128)}, f32[24,65536]{1,0:T(8,128)}, f32[24,65536]{1,0:T(8,128)}, bf16[4,4,128,4,128]{2,4,3,1,0:T(8,128)(2,1)}, s32[4,4,8]{2,1,0:T(4,128)S(...) while((s32[]{:T(128)}, f32[24,65536]{1,0:T(8,128)}, ...), condition=%wide.region_7.8_spmd.clone, body=%wide.region_6.7_spmd.clone.sunk | while | flops 3921678336 | bytes 274790528 | solution.py:171
  264.8 9.9 %copy.124 = f32[4,8,128,4,128]{4,3,2,1,0:T(4,128)} copy(f32[4,8,128,4,128]{2,4,1,3,0:T(8,128)} %fusion.116) | data formatting | bytes 16777216 | tf_op jit(solution)/shard_map/while/body/eval_jaxpr/bhqek,bqhd->bekhd/transpose | solution.py:154
  274.8 9.0 %reshape.299 = f32[32,65536]{1,0:T(8,128)} reshape(f32[4,8,128,4,128]{4,3,2,1,0:T(4,128)} %copy.124) | data formatting | bytes 16777216 | tf_op jit(solution)/shard_map/while/body/eval_jaxpr/reshape | solution.py:166
  283.8 8.2 %convolution_add_fusion.6 = f32[24,65536]{1,0:T(8,128)} fusion(f32[32,65536]{1,0:T(8,128)} %reshape.299, f32[24,65536]{1,0:T(8,128)} %get-tuple-element.489, pred[]{:T(512)S(6)} %compare.14, s32[32]{0:T(128)S(1)} %eq.72, pred[32]{0:T(512)(128)(4,1)S(1)} %and.73), kind=kOutput, calls=%fused_computation.30.clone.1 | convolution fusion | flops 607127040 | bytes 20971680 | tf_op jit(solution)/shard_map/while/body/eval_jaxpr/dot_general | solution.py:165
  297.6 9.9 %copy.123 = f32[4,8,128,4,128]{4,3,2,1,0:T(4,128)} copy(f32[4,8,128,4,128]{2,4,1,3,0:T(8,128)} %convolution_bitcast_fusion.3) | data formatting | bytes 16777216 | tf_op jit(solution)/shard_map/while/body/eval_jaxpr/bhqek,bqhd->bekhd/transpose | solution.py:151
  307.5 9.0 %reshape.298 = f32[32,65536]{1,0:T(8,128)} reshape(f32[4,8,128,4,128]{4,3,2,1,0:T(4,128)} %copy.123) | data formatting | bytes 16777216 | tf_op jit(solution)/shard_map/while/body/eval_jaxpr/reshape | solution.py:163
  316.6 8.0 %convolution_add_fusion.5 = f32[24,65536]{1,0:T(8,128)} fusion(f32[32,65536]{1,0:T(8,128)} %reshape.298, f32[24,65536]{1,0:T(8,128)} %get-tuple-element.488, pred[]{:T(512)S(6)} %compare.14, s32[32]{0:T(128)S(1)} %eq.72, pred[32]{0:T(512)(128)(4,1)S(1)} %and.73), kind=kOutput, calls=%fused_computation.31.clone.1 | convolution fusion | flops 607127040 | bytes 20971680 | tf_op jit(solution)/shard_map/while/body/eval_jaxpr/dot_general | solution.py:162
  361.8 9.9 %copy.124 = f32[4,8,128,4,128]{4,3,2,1,0:T(4,128)} copy(f32[4,8,128,4,128]{2,4,1,3,0:T(8,128)} %fusion.116) | data formatting | bytes 16777216 | tf_op jit(solution)/shard_map/while/body/eval_jaxpr/bhqek,bqhd->bekhd/transpose | solution.py:154
  371.7 9.0 %reshape.299 = f32[32,65536]{1,0:T(8,128)} reshape(f32[4,8,128,4,128]{4,3,2,1,0:T(4,128)} %copy.124) | data formatting | bytes 16777216 | tf_op jit(solution)/shard_map/while/body/eval_jaxpr/reshape | solution.py:166
  380.7 9.2 %convolution_add_fusion.6 = f32[24,65536]{1,0:T(8,128)} fusion(f32[32,65536]{1,0:T(8,128)} %reshape.299, f32[24,65536]{1,0:T(8,128)} %get-tuple-element.489, pred[]{:T(512)S(6)} %compare.14, s32[32]{0:T(128)S(1)} %eq.72, pred[32]{0:T(512)(128)(4,1)S(1)} %and.73), kind=kOutput, calls=%fused_computation.30.clone.1 | convolution fusion | flops 607127040 | bytes 20971680 | tf_op jit(solution)/shard_map/while/body/eval_jaxpr/dot_general | solution.py:165
  395.5 9.9 %copy.123 = f32[4,8,128,4,128]{4,3,2,1,0:T(4,128)} copy(f32[4,8,128,4,128]{2,4,1,3,0:T(8,128)} %convolution_bitcast_fusion.3) | data formatting | bytes 16777216 | tf_op jit(solution)/shard_map/while/body/eval_jaxpr/bhqek,bqhd->bekhd/transpose | solution.py:151
  405.4 9.0 %reshape.298 = f32[32,65536]{1,0:T(8,128)} reshape(f32[4,8,128,4,128]{4,3,2,1,0:T(4,128)} %copy.123) | data formatting | bytes 16777216 | tf_op jit(solution)/shard_map/while/body/eval_jaxpr/reshape | solution.py:163
  414.4 9.0 %convolution_add_fusion.5 = f32[24,65536]{1,0:T(8,128)} fusion(f32[32,65536]{1,0:T(8,128)} %reshape.298, f32[24,65536]{1,0:T(8,128)} %get-tuple-element.488, pred[]{:T(512)S(6)} %compare.14, s32[32]{0:T(128)S(1)} %eq.72, pred[32]{0:T(512)(128)(4,1)S(1)} %and.73), kind=kOutput, calls=%fused_computation.31.clone.1 | convolution fusion | flops 607127040 | bytes 20971680 | tf_op jit(solution)/shard_map/while/body/eval_jaxpr/dot_general | solution.py:162
  460.6 9.9 %copy.124 = f32[4,8,128,4,128]{4,3,2,1,0:T(4,128)} copy(f32[4,8,128,4,128]{2,4,1,3,0:T(8,128)} %fusion.116) | data formatting | bytes 16777216 | tf_op jit(solution)/shard_map/while/body/eval_jaxpr/bhqek,bqhd->bekhd/transpose | solution.py:154
  470.5 9.0 %reshape.299 = f32[32,65536]{1,0:T(8,128)} reshape(f32[4,8,128,4,128]{4,3,2,1,0:T(4,128)} %copy.124) | data formatting | bytes 16777216 | tf_op jit(solution)/shard_map/while/body/eval_jaxpr/reshape | solution.py:166
  479.6 9.2 %convolution_add_fusion.6 = f32[24,65536]{1,0:T(8,128)} fusion(f32[32,65536]{1,0:T(8,128)} %reshape.299, f32[24,65536]{1,0:T(8,128)} %get-tuple-element.489, pred[]{:T(512)S(6)} %compare.14, s32[32]{0:T(128)S(1)} %eq.72, pred[32]{0:T(512)(128)(4,1)S(1)} %and.73), kind=kOutput, calls=%fused_computation.30.clone.1 | convolution fusion | flops 607127040 | bytes 20971680 | tf_op jit(solution)/shard_map/while/body/eval_jaxpr/dot_general | solution.py:165
  494.4 9.9 %copy.123 = f32[4,8,128,4,128]{4,3,2,1,0:T(4,128)} copy(f32[4,8,128,4,128]{2,4,1,3,0:T(8,128)} %convolution_bitcast_fusion.3) | data formatting | bytes 16777216 | tf_op jit(solution)/shard_map/while/body/eval_jaxpr/bhqek,bqhd->bekhd/transpose | solution.py:151
  504.3 9.0 %reshape.298 = f32[32,65536]{1,0:T(8,128)} reshape(f32[4,8,128,4,128]{4,3,2,1,0:T(4,128)} %copy.123) | data formatting | bytes 16777216 | tf_op jit(solution)/shard_map/while/body/eval_jaxpr/reshape | solution.py:163
  513.3 9.0 %convolution_add_fusion.5 = f32[24,65536]{1,0:T(8,128)} fusion(f32[32,65536]{1,0:T(8,128)} %reshape.298, f32[24,65536]{1,0:T(8,128)} %get-tuple-element.488, pred[]{:T(512)S(6)} %compare.14, s32[32]{0:T(128)S(1)} %eq.72, pred[32]{0:T(512)(128)(4,1)S(1)} %and.73), kind=kOutput, calls=%fused_computation.31.clone.1 | convolution fusion | flops 607127040 | bytes 20971680 | tf_op jit(solution)/shard_map/while/body/eval_jaxpr/dot_general | solution.py:162
  559.5 9.9 %copy.124 = f32[4,8,128,4,128]{4,3,2,1,0:T(4,128)} copy(f32[4,8,128,4,128]{2,4,1,3,0:T(8,128)} %fusion.116) | data formatting | bytes 16777216 | tf_op jit(solution)/shard_map/while/body/eval_jaxpr/bhqek,bqhd->bekhd/transpose | solution.py:154
  569.4 9.0 %reshape.299 = f32[32,65536]{1,0:T(8,128)} reshape(f32[4,8,128,4,128]{4,3,2,1,0:T(4,128)} %copy.124) | data formatting | bytes 16777216 | tf_op jit(solution)/shard_map/while/body/eval_jaxpr/reshape | solution.py:166
  578.4 9.2 %convolution_add_fusion.6 = f32[24,65536]{1,0:T(8,128)} fusion(f32[32,65536]{1,0:T(8,128)} %reshape.299, f32[24,65536]{1,0:T(8,128)} %get-tuple-element.489, pred[]{:T(512)S(6)} %compare.14, s32[32]{0:T(128)S(1)} %eq.72, pred[32]{0:T(512)(128)(4,1)S(1)} %and.73), kind=kOutput, calls=%fused_computation.30.clone.1 | convolution fusion | flops 607127040 | bytes 20971680 | tf_op jit(solution)/shard_map/while/body/eval_jaxpr/dot_general | solution.py:165
  593.2 9.9 %copy.123 = f32[4,8,128,4,128]{4,3,2,1,0:T(4,128)} copy(f32[4,8,128,4,128]{2,4,1,3,0:T(8,128)} %convolution_bitcast_fusion.3) | data formatting | bytes 16777216 | tf_op jit(solution)/shard_map/while/body/eval_jaxpr/bhqek,bqhd->bekhd/transpose | solution.py:151
  603.1 9.0 %reshape.298 = f32[32,65536]{1,0:T(8,128)} reshape(f32[4,8,128,4,128]{4,3,2,1,0:T(4,128)} %copy.123) | data formatting | bytes 16777216 | tf_op jit(solution)/shard_map/while/body/eval_jaxpr/reshape | solution.py:163
  612.2 9.0 %convolution_add_fusion.5 = f32[24,65536]{1,0:T(8,128)} fusion(f32[32,65536]{1,0:T(8,128)} %reshape.298, f32[24,65536]{1,0:T(8,128)} %get-tuple-element.488, pred[]{:T(512)S(6)} %compare.14, s32[32]{0:T(128)S(1)} %eq.72, pred[32]{0:T(512)(128)(4,1)S(1)} %and.73), kind=kOutput, calls=%fused_computation.31.clone.1 | convolution fusion | flops 607127040 | bytes 20971680 | tf_op jit(solution)/shard_map/while/body/eval_jaxpr/dot_general | solution.py:162
  647.9 8.4 %slice.127 = f32[16,131072]{1,0:T(8,128)} slice(f32[24,131072]{1,0:T(8,128)} %constant_dynamic-update-slice_fusion.2), slice={[3:19], [0:131072]} | slice | bytes 16777216 | tf_op jit(solution)/shard_map/slice | solution.py:187
  667.0 20.5 %scatter-add.6 = f32[16,131072]{1,0:T(8,128)} dynamic-update-slice(f32[16,131072]{1,0:T(8,128)} %slice.127, f32[3,131072]{1,0:T(4,128)S(1)} %convert_add_fusion, s32[]{:T(128)} %constant.123.clone.1, s32[]{:T(128)} %constant.123.clone.1) | dynamic-update-slice | bytes 3145732 | tf_op jit(solution)/shard_map/scatter-add | solution.py:190
  691.8 13.4 %scatter-add.9 = f32[16,131072]{1,0:T(8,128)} dynamic-update-slice(f32[16,131072]{1,0:T(8,128)} %scatter-add.6, f32[3,131072]{1,0:T(4,128)S(1)} %slice_add_fusion, s32[]{:T(128)} %constant.133.clone.1, s32[]{:T(128)} %constant.123.clone.1) | dynamic-update-slice | bytes 3145732 | tf_op jit(solution)/shard_map/scatter-add | solution.py:191
  705.2 9.9 %all-reduce.3.cloned.1.call-done = f32[2,131072]{1,0:T(2,128)} async-done(((f32[2,131072]{1,0:T(2,128)}), f32[2,131072]{1,0:T(2,128)}) %all-reduce.3.cloned.1.call-update) | async-done | bytes 1048592 | tf_op jit(solution)/shard_map/psum | solution.py:192
  (241 shorter events, 395.9 us)
Async XLA Ops:
  7.2 3.3 copy-start.7
  7.2 85.5 %all-gather.4.cloned.1.call-start = ((), (), s32[]{:S(2)}) async-start(), calls=%async_computation.1 | async-start | bytes 2621440 | tf_op jit(solution)/shard_map/all_gather | solution.py:84
  11.9 4.8 copy-start.11
  16.8 6.7 copy-start.9
  16.8 13.0 %copy-start.8 = (s32[64,6]{0,1:T(8,128)S(1)}, s32[64,6]{0,1:T(8,128)}, u32[]{:S(2)}) copy-start(s32[64,6]{0,1:T(8,128)} %param.19) | copy-start | bytes 4612
  16.8 13.3 %copy-start.6 = (bf16[2048,512]{1,0:T(8,128)(2,1)S(1)}, bf16[2048,512]{1,0:T(8,128)(2,1)}, u32[]{:S(2)}) copy-start(bf16[2048,512]{1,0:T(8,128)(2,1)} %param.17) | copy-start | bytes 6291460
  20.8 694.4 %all-reduce.3.cloned.1.call-start = ((), (), s32[]{:S(2)}) async-start(), calls=%async_computation | async-start | bytes 2097152 | tf_op jit(solution)/shard_map/psum | solution.py:192
  23.5 36.7 %collective-permute-start = (bf16[384,1024]{1,0:T(8,128)(2,1)}, bf16[384,1024]{1,0:T(8,128)(2,1)S(1)}, u32[]{:S(2)}, u32[]{:S(2)}) collective-permute-start(bf16[384,1024]{1,0:T(8,128)(2,1)} %get-tuple-element.302), channel_id=1, source_target_pairs={{0,8},{8,16},{16,24},{1,9},{9,17},{17,25},{2,10},{10,18},{18,26},{... | collective-permute-start | bytes 2359304 | tf_op jit(solution)/shard_map/ppermute | solution.py:21
  28.5 54.8 %collective-permute-start.1 = (bf16[384,1024]{1,0:T(8,128)(2,1)}, bf16[384,1024]{1,0:T(8,128)(2,1)}, u32[]{:S(2)}, u32[]{:S(2)}) collective-permute-start(bf16[384,1024]{1,0:T(8,128)(2,1)} %get-tuple-element.303), channel_id=1, source_target_pairs={{8,0},{16,8},{24,16},{9,1},{17,9},{25,17},{10,2},{18,10},{26,18},{... | collective-permute-start | bytes 2359304 | tf_op jit(solution)/shard_map/ppermute | solution.py:23
  132.0 2.2 copy-start.3
  206.6 2.2 copy-start.3
  250.9 3.7 copy-start.4
  250.9 3.8 copy-start.5
  254.6 3.5 copy-start
  283.8 8.3 %copy-start.2 = (bf16[4,4,128,8,128]{4,2,3,1,0:T(8,128)(2,1)S(1)}, bf16[4,4,128,8,128]{4,2,3,1,0:T(8,128)(2,1)}, u32[]{:S(2)}) copy-start(bf16[4,4,128,8,128]{4,2,3,1,0:T(8,128)(2,1)} %copy-done.1) | copy-start | bytes 12582916 | tf_op jit(solution)/shard_map/while
  347.8 3.7 copy-start.4
  347.8 3.8 copy-start.5
  351.6 3.5 copy-start
  380.7 9.2 %copy-start.2 = (bf16[4,4,128,8,128]{4,2,3,1,0:T(8,128)(2,1)S(1)}, bf16[4,4,128,8,128]{4,2,3,1,0:T(8,128)(2,1)}, u32[]{:S(2)}) copy-start(bf16[4,4,128,8,128]{4,2,3,1,0:T(8,128)(2,1)} %copy-done.1) | copy-start | bytes 12582916 | tf_op jit(solution)/shard_map/while
  446.7 3.7 copy-start.4
  446.7 3.8 copy-start.5
  450.4 3.5 copy-start
  479.6 9.2 %copy-start.2 = (bf16[4,4,128,8,128]{4,2,3,1,0:T(8,128)(2,1)S(1)}, bf16[4,4,128,8,128]{4,2,3,1,0:T(8,128)(2,1)}, u32[]{:S(2)}) copy-start(bf16[4,4,128,8,128]{4,2,3,1,0:T(8,128)(2,1)} %copy-done.1) | copy-start | bytes 12582916 | tf_op jit(solution)/shard_map/while
  545.5 3.7 copy-start.4
  545.5 3.8 copy-start.5
  549.3 3.5 copy-start
  578.4 9.2 %copy-start.2 = (bf16[4,4,128,8,128]{4,2,3,1,0:T(8,128)(2,1)S(1)}, bf16[4,4,128,8,128]{4,2,3,1,0:T(8,128)(2,1)}, u32[]{:S(2)}) copy-start(bf16[4,4,128,8,128]{4,2,3,1,0:T(8,128)(2,1)} %copy-done.1) | copy-start | bytes 12582916 | tf_op jit(solution)/shard_map/while
  621.4 6.1 slice-start
  621.4 6.1 slice-start.1
  637.9 25.0 %collective-permute-start.2 = (bf16[3,131072]{1,0:T(4,128)(2,1)}, bf16[3,131072]{1,0:T(4,128)(2,1)S(1)}, u32[]{:S(2)}, u32[]{:S(2)}) collective-permute-start(bf16[3,131072]{1,0:T(4,128)(2,1)} %get-tuple-element.296), channel_id=1, source_target_pairs={{0,8},{8,16},{16,24},{1,9},{9,17},{17,25},{2,10},{10,18},{18,26},{... | collective-permute-start | bytes 2359304 | tf_op jit(solution)/shard_map/ppermute | solution.py:21
  639.9 22.9 %collective-permute-start.3 = (bf16[3,131072]{1,0:T(4,128)(2,1)}, bf16[3,131072]{1,0:T(4,128)(2,1)}, u32[]{:S(2)}, u32[]{:S(2)}) collective-permute-start(bf16[3,131072]{1,0:T(4,128)(2,1)} %get-tuple-element.297), channel_id=1, source_target_pairs={{8,0},{16,8},{24,16},{9,1},{17,9},{25,17},{10,2},{18,10},{26,18},{... | collective-permute-start | bytes 2359304 | tf_op jit(solution)/shard_map/ppermute | solution.py:23
  691.8 23.4 %copy-start.10 = (s32[2]{0:T(128)S(1)}, s32[2]{0:T(128)}, u32[]{:S(2)}) copy-start(s32[2]{0:T(128)} %copy-done.9) | copy-start | bytes 28
  (6 other events, 13.1 us)
Sparse Core Ops, SparseCore 0:
  20.9 63.6 all-gather.3
  662.9 52.1 all-reduce.2
